TPU v7x, 32 devices: a whole 2x2x4 slice. The times are simulated.
32 devices in a mesh: sec: 8 (over y, x, core), col: 4 (over z).
Axes of the slice: x: 2, y: 2, z: 4, core: 2. Of those that a mesh axis runs over, the one named last changes fastest.
Arguments:
- air_state: float32 [4, 64, 32768], P(None, None, ('sec', 'col')), may hold values from -6 to 6
- air_mix: float32 [64, 32768], P(None, ('sec', 'col')), may hold values from 0.1 to 4
- surface_forcing: float32 [4, 32768], P(None, ('sec', 'col')), may hold values from 0 to 2
- air_mask: int32 [32768], P(('sec', 'col')), may hold values 0 or 1
- ocean_sources: int32 [4, 32768], P(None, ('sec', 'col')), may hold values from 0 to 6143, as said below
- ocean_weights: float32 [4, 32768], P(None, ('sec', 'col')), may hold values from 0.1 to 0.5
- sea_state: float32 [2, 80, 16384], P(None, None, ('sec', 'col')), may hold values from -6 to 6
- sea_mix: float32 [80, 16384], P(None, ('sec', 'col')), may hold values from 0.1 to 4
- ice_cover: float32 [16384], P(('sec', 'col')), may hold values from 0.05 to 0.95
- sea_mask: int32 [16384], P(('sec', 'col')), may hold values 0 or 1
- air_sources: int32 [4, 16384], P(None, ('sec', 'col')), may hold values from 0 to 12287, as said below
- air_weights: float32 [4, 16384], P(None, ('sec', 'col')), may hold values from 0.1 to 0.5
Outputs:
- air_out: float32 [4, 64, 32768], P(None, None, ('sec', 'col'))
- sea_out: float32 [2, 80, 16384], P(None, None, ('sec', 'col'))
- ice_out: float32 [16384], P(('sec', 'col'))
Inputs may be any that keep to these rules, and one draw needn't show every extreme that they name: Section t holds ocean cells t * 2048 to (t + 1) * 2048 - 1 and atmosphere columns t * 4096 to (t + 1) * 4096 - 1. An entry s of ocean_sources names cell s mod 2048 of the section s // 2048 - 1 places after the column's own. An entry s of air_sources names column s mod 4096 of the section s // 4096 - 1 places after the cell's own.
All inputs are finite; a program needn't handle non-finite values. No bound on the sum of `air_mask` or of `sea_mask` on one device may be relied on, other than what follows from the above.
Results may differ from a plain program's by a relative error of at most 0.0001.
Values sent between devices are 32-bit elements; how exact they have to be, the bound alone decides.
No kernel may reach another device: no remote copies, remote signals or barrier semaphores. Data moves between devices by JAX's collectives and lax.ppermute only.
A program may use at most 64 MiB of HBM per device.

v0:
```python
import jax
import jax.numpy as jnp
from jax import lax
from jax.sharding import PartitionSpec as P

STEPS = 2


def extended(value, sides, width):
    for axis, dim in sides:
        peers, length = (lax.axis_size(axis), value.shape[dim])
        up = [(i, (i + 1) % peers) for i in range(peers)]
        down = [(j, i) for i, j in up]
        last = lax.slice_in_dim(value, length - width, length, axis=dim)
        leading = lax.slice_in_dim(value, 0, width, axis=dim)
        before = lax.ppermute(last, axis, up)
        after = lax.ppermute(leading, axis, down)
        value = jnp.concatenate([before, value, after], axis=dim)
    return value


def solve_columns(mixing, right_side):
    column_depth = mixing.shape[0]
    zeros_row = jnp.zeros_like(mixing[0])
    carry_c = zeros_row
    carry_d = jnp.zeros_like(right_side[:, 0])
    ratios = []
    reduced = []
    for depth_index in range(column_depth):
        lower_k = mixing[depth_index - 1] if depth_index > 0 else zeros_row
        upper_k = mixing[depth_index]
        pivot_value = 1.0 + lower_k + upper_k + lower_k * carry_c
        carry_c = -upper_k / pivot_value
        carry_d = (right_side[:, depth_index] + lower_k * carry_d) / pivot_value
        ratios.append(carry_c)
        reduced.append(carry_d)
    current = reduced[-1]
    solved = [current]
    for depth_index in range(column_depth - 2, -1, -1):
        current = reduced[depth_index] - ratios[depth_index] * current
        solved.append(current)
    return jnp.stack(solved[::-1], axis=1)


def remap(values, places, weights):
    return jnp.sum(weights[None] * values[:, places], axis=1)


def surface_fluxes(air_state, air_sea, surface_forcing, air_mask):
    bottom = air_state[:, 0]
    over_sea = air_mask == 1
    skin = jnp.where(over_sea, air_sea[0], surface_forcing[3])
    frozen = jnp.where(over_sea, air_sea[1], 0.0)
    speed = jnp.sqrt(bottom[2] * bottom[2] + bottom[3] * bottom[3] + 1.0)
    coefficient = 0.3 * speed / (1.0 + frozen)
    snow_part = 1.0 / (1.0 + jnp.exp(2.0 * skin))
    return jnp.stack(
        [
            coefficient * (skin - bottom[0]),
            coefficient * (0.5 * jnp.exp(0.3 * skin) - bottom[1]),
            coefficient * bottom[2],
            coefficient * bottom[3],
            surface_forcing[0] / (1.0 + frozen),
            surface_forcing[1] - 0.2 * skin,
            surface_forcing[2] * (1.0 - snow_part),
            surface_forcing[2] * snow_part,
        ]
    )


def air_step(air_state, air_mix, fluxes):
    bottom_add = jnp.stack([fluxes[0], fluxes[1], -fluxes[2], -fluxes[3]])
    return solve_columns(air_mix, air_state.at[:, 0].add(bottom_add))


def sea_step(sea_state, sea_mix, ice_cover, sea_mask, sea_flux):
    stress = jnp.sqrt(sea_flux[2] * sea_flux[2] + sea_flux[3] * sea_flux[3] + 0.01)
    heat = sea_flux[4] + sea_flux[5] - sea_flux[0] - sea_flux[1]
    open_water = 1.0 - ice_cover
    depth_decay = jnp.exp(-jnp.arange(sea_mix.shape[0], dtype=jnp.float32) / 8.0)
    mixing = sea_mix * (1.0 + 2.0 * stress[None, :] * depth_decay[:, None])
    top_add = jnp.stack(
        [0.5 * open_water * heat, 0.3 * open_water * (0.4 * sea_flux[1] - sea_flux[6])]
    )
    solved = solve_columns(mixing, sea_state.at[:, 0].add(top_add))
    wet_cells = sea_mask == 1
    new_state = jnp.where(wet_cells[None, None], solved, sea_state)
    grown = ice_cover / (ice_cover + open_water * jnp.exp(0.5 * heat - 0.8 * sea_flux[7]))
    return (new_state, jnp.where(wet_cells, grown, ice_cover))


def per_device(
    air_state,
    air_mix,
    surface_forcing,
    air_mask,
    ocean_sources,
    ocean_weights,
    sea_state,
    sea_mix,
    ice_cover,
    sea_mask,
    air_sources,
    air_weights,
):
    group_count = lax.axis_size("col")
    air_cols = air_state.shape[2]
    sea_cols = sea_state.shape[2]
    air_span = air_cols * group_count
    for step_index in range(STEPS):
        sea_top = jnp.stack([sea_state[0, 0], ice_cover])
        sea_block = lax.all_gather(sea_top, "col", axis=1, tiled=True)
        sea_nearby = extended(sea_block, (("sec", 1),), sea_cols * group_count)
        air_sea = remap(sea_nearby, ocean_sources, ocean_weights)
        fluxes = surface_fluxes(air_state, air_sea, surface_forcing, air_mask)
        flux_block = lax.all_gather(fluxes, "col", axis=1, tiled=True)
        flux_nearby = extended(flux_block, (("sec", 1),), air_span)
        air_state = air_step(air_state, air_mix, fluxes)
        sea_flux = remap(flux_nearby, air_sources, air_weights)
        sea_state, ice_cover = sea_step(sea_state, sea_mix, ice_cover, sea_mask, sea_flux)
    return (air_state, sea_state, ice_cover)


def solution(mesh):
    placed = (
        P(None, None, ("sec", "col")),
        P(None, ("sec", "col")),
        P(None, ("sec", "col")),
        P(("sec", "col")),
        P(None, ("sec", "col")),
        P(None, ("sec", "col")),
        P(None, None, ("sec", "col")),
        P(None, ("sec", "col")),
        P(("sec", "col")),
        P(("sec", "col")),
        P(None, ("sec", "col")),
        P(None, ("sec", "col")),
    )
    return jax.shard_map(
        per_device,
        mesh=mesh,
        in_specs=placed,
        out_specs=(P(None, None, ("sec", "col")), P(None, None, ("sec", "col")), P(("sec", "col"))),
        check_vma=False,
    )
```

profile of v0, /device:TPU:0, one launch (start us, length us, event | category | flops | bytes accessed | tf_op | source)
XLA Modules:
  0.0 243.3 jit_solution(5167946704040412479)
XLA Ops:
  2.1 14.9 %all_gather.12 = f32[2,2048]{1,0:T(2,128)S(1)} all-gather(f32[2,512]{1,0:T(2,128)S(1)} %pad_maximum_fusion.4), channel_id=1, replica_groups=mesh['sec'=8,'col'=4] {'col'}, dimensions={1}, use_global_device_ids=true | all-gather | bytes 20480 | tf_op jit(solution)/shard_map/all_gather | solution.py:112
  17.5 1.9 fusion.457
  19.5 1.9 fusion.458
  21.5 1.8 fusion.459
  23.3 2.9 %negate_divide_fusion.20 = (f32[1,1024]{1,0:T(1,128)}, f32[1,1024]{1,0:T(1,128)}, f32[1,1024]{1,0:T(1,128)}, f32[1,1024]{1,0:T(1,128)}, f32[1,1024]{1,0:T(1,128)...) fusion(f32[64,1024]{1,0:T(8,128)} %param.21), kind=kLoop, calls=%fused_computation.1316 | loop fusion | flops 260096 | bytes 524288 | tf_op jit(solution)/shard_map/div | solution.py:33
  26.2 3.2 %fusion.452 = (f32[4,1,1024]{2,1,0:T(1,128)S(1)}, f32[4,1,1024]{2,1,0:T(1,128)}, f32[4,1,1024]{2,1,0:T(1,128)}, f32[4,1,1024]{2,1,0:T(1,128)}, f32[4,1,1024]{2,1...) fusion(f32[4,64,1024]{2,1,0:T(8,128)} %param.20), kind=kLoop, calls=%fused_computation.1762 | loop fusion | bytes 622592 | tf_op jit(solution)/shard_map/slice | solution.py:34
  29.4 3.4 %fusion.453 = (f32[4,1,1024]{2,1,0:T(1,128)}, f32[4,1,1024]{2,1,0:T(1,128)}, f32[4,1,1024]{2,1,0:T(1,128)}, f32[4,1,1024]{2,1,0:T(1,128)}, f32[4,1,1024]{2,1,0:T...) fusion(f32[4,64,1024]{2,1,0:T(8,128)} %param.20), kind=kLoop, calls=%fused_computation.1763 | loop fusion | bytes 622592 | tf_op jit(solution)/shard_map/slice | solution.py:34
  32.9 1.9 fusion.456
  36.4 2.3 fusion.454
  38.7 3.3 %fusion.451 = (f32[4,1,1024]{2,1,0:T(1,128)}, f32[4,1,1024]{2,1,0:T(1,128)S(1)}, f32[4,1,1024]{2,1,0:T(1,128)}, f32[4,1,1024]{2,1,0:T(1,128)}, f32[4,1,1024]{2,1...) fusion(f32[4,64,1024]{2,1,0:T(8,128)} %param.20), kind=kLoop, calls=%fused_computation.1761 | loop fusion | bytes 622592 | tf_op jit(solution)/shard_map/slice | solution.py:34
  43.8 1.7 multiply_add_fusion.20
  72.4 1.8 copy.754
  74.1 15.4 %gather_fusion = f32[4096,2]{1,0:T(8,128)} fusion(f32[2,6144]{0,1:T(8,128)S(1)} %copy.754, s32[4096]{0:T(1024)} %bitcast_clamp_fusion), kind=kCustom, calls=%fused_computation | custom fusion | bytes 81920 | tf_op jit(solution)/shard_map/gather | solution.py:46
  89.9 2.0 multiply_reduce_fusion.1
  94.7 13.5 %all_gather.13 = f32[8,4096]{1,0:T(8,128)S(1)} all-gather(f32[8,1024]{1,0:T(8,128)S(1)} %stack.715), channel_id=1, replica_groups=mesh['sec'=8,'col'=4] {'col'}, dimensions={1}, use_global_device_ids=true | all-gather | bytes 163840 | tf_op jit(solution)/shard_map/all_gather | solution.py:116
  109.1 1.9 fusion.91
  111.4 3.7 %multiply_subtract_fusion.103 = (f32[4,1024]{1,0:T(4,128)S(1)}, f32[4,1024]{1,0:T(4,128)}, f32[4,1024]{1,0:T(4,128)}, f32[4,1024]{1,0:T(4,128)}, f32[4,1024]{1,0...) fusion(f32[4,1024]{1,0:T(4,128)S(1)} %get-tuple-element.742, ...), kind=kLoop, calls=%fused_computation.712 | loop fusion | flops 1200128 | bytes 2097152 | tf_op jit(solution)/shard_map/sub | solution.py:40
  115.5 2.2 add_divide_fusion.63
  117.8 3.9 %copy.819 = f32[8,12288]{0,1:T(8,128)} copy(f32[8,12288]{1,0:T(8,128)S(1)} %pad_maximum_fusion) | data formatting | bytes 786432 | tf_op jit(solution)/shard_map/concatenate | solution.py:18
  121.7 8.3 %gather_fusion.1 = f32[2048,8]{1,0:T(8,128)S(1)} fusion(f32[8,12288]{0,1:T(8,128)} %copy.819, s32[2048]{0:T(1024)S(1)} %copy-done.205), kind=kCustom, calls=%fused_computation.1 | custom fusion | bytes 139264 | tf_op jit(solution)/shard_map/gather | solution.py:46
  135.8 13.2 %all_gather.14 = f32[2,2048]{1,0:T(2,128)S(1)} all-gather(f32[2,512]{1,0:T(2,128)S(1)} %pad_maximum_fusion.5), channel_id=1, replica_groups=mesh['sec'=8,'col'=4] {'col'}, dimensions={1}, use_global_device_ids=true | all-gather | bytes 20480 | tf_op jit(solution)/shard_map/all_gather | solution.py:112
  150.5 2.7 %collective-permute-done.4 = f32[2,2048]{1,0:T(2,128)S(1)} collective-permute-done((f32[2,2048]{1,0:T(2,128)S(1)}, f32[2,2048]{1,0:T(2,128)S(1)}, u32[]{:S(2)}, u32[]{:S(2)}) %collective-permute-start.4) | collective-permute-done | bytes 16416 | tf_op jit(solution)/shard_map/ppermute | solution.py:16
  153.9 1.8 copy.901
  155.6 15.4 %gather_fusion.2 = f32[4096,2]{1,0:T(8,128)} fusion(f32[2,6144]{0,1:T(8,128)S(1)} %copy.901, s32[4096]{0:T(1024)} %bitcast_clamp_fusion), kind=kCustom, calls=%fused_computation.2 | custom fusion | bytes 81920 | tf_op jit(solution)/shard_map/gather | solution.py:46
  171.4 2.0 multiply_reduce_fusion
  176.2 13.5 %all_gather.15 = f32[8,4096]{1,0:T(8,128)S(1)} all-gather(f32[8,1024]{1,0:T(8,128)S(1)} %stack.831), channel_id=1, replica_groups=mesh['sec'=8,'col'=4] {'col'}, dimensions={1}, use_global_device_ids=true | all-gather | bytes 163840 | tf_op jit(solution)/shard_map/all_gather | solution.py:116
  190.5 3.1 %add_divide_fusion.38 = (f32[4,1,1024]{2,0,1:T(4,128)S(1)}, f32[4,1,1024]{2,0,1:T(4,128)S(1)}, f32[4,1,1024]{2,0,1:T(4,128)S(1)}, f32[4,1,1024]{2,0,1:T(4,128)S(...) fusion(f32[1024]{0:T(1024)} %bitcast.3545, ...), kind=kLoop, calls=%fused_computation.586 | loop fusion | flops 1093632 | bytes 2232320 | tf_op jit(solution)/shard_map/div | solution.py:34
  193.9 2.0 add_divide_fusion.60
  196.0 2.6 %constant_dynamic-update-slice_fusion.143 = (f32[4,64,1024]{2,0,1:T(4,128)S(1)}, f32[4,1024]{1,0:T(4,128)S(1)}, f32[4,1024]{1,0:T(4,128)S(1)}, f32[4,1024]{1,0:T...) fusion(f32[4,1024]{1,0:T(4,128)S(1)} %get-tuple-element.437, ...), kind=kLoop, calls=%fused_computation.155 | loop fusion | flops 1392639 | bytes 2138112
  199.0 3.4 %constant_dynamic-update-slice_fusion.142 = (f32[4,64,1024]{2,0,1:T(4,128)S(1)}, f32[4,1,1024]{2,0,1:T(4,128)S(1)}, f32[4,1,1024]{2,0,1:T(4,128)S(1)}, f32[4,1,1...) fusion(f32[4,64,1024]{2,0,1:T(4,128)S(1)} %get-tuple-element.40, ...), kind=kLoop, calls=%fused_computation.154 | loop fusion | flops 1454080 | bytes 2519040
  223.9 4.2 %copy.902 = f32[8,12288]{0,1:T(8,128)} copy(f32[8,12288]{1,0:T(8,128)S(1)} %pad_maximum_fusion.1) | data formatting | bytes 786432 | tf_op jit(solution)/shard_map/concatenate | solution.py:18
  228.1 8.3 %gather_fusion.3 = f32[2048,8]{1,0:T(8,128)S(1)} fusion(f32[8,12288]{0,1:T(8,128)} %copy.902, s32[2048]{0:T(1024)S(1)} %copy-done.206), kind=kCustom, calls=%fused_computation.3 | custom fusion | bytes 139264 | tf_op jit(solution)/shard_map/gather | solution.py:46
  (830 shorter events, 73.8 us)
Async XLA Ops:
  17.0 54.5 %collective-permute-start.1 = (f32[2,2048]{1,0:T(2,128)S(1)}, f32[2,2048]{1,0:T(2,128)S(1)}, u32[]{:S(2)}, u32[]{:S(2)}) collective-permute-start(f32[2,2048]{1,0:T(2,128)S(1)} %all_gather.12), channel_id=1, source_target_pairs={{4,0},{8,4},{12,8},{16,12},{20,16},{24,20},{28,24},{0,28},{5,1},{9... | collective-permute-start | bytes 49160 | tf_op jit(solution)/shard_map/ppermute | solution.py:17
  17.0 54.6 %collective-permute-start = (f32[2,2048]{1,0:T(2,128)S(1)}, f32[2,2048]{1,0:T(2,128)S(1)}, u32[]{:S(2)}, u32[]{:S(2)}) collective-permute-start(f32[2,2048]{1,0:T(2,128)S(1)} %all_gather.12), channel_id=1, source_target_pairs={{0,4},{4,8},{8,12},{12,16},{16,20},{20,24},{24,28},{28,0},{1,5},{5... | collective-permute-start | bytes 49160 | tf_op jit(solution)/shard_map/ppermute | solution.py:16
  19.4 51.9 %copy-start.50 = (f32[1,1024]{1,0:T(1,128)}, f32[1,1024]{1,0:T(1,128)S(1)}, u32[]{:S(2)}) copy-start(f32[1,1024]{1,0:T(1,128)S(1)} %get-tuple-element.988) | copy-start | bytes 12292
  19.4 51.9 %copy-start.53 = (f32[1,1024]{1,0:T(1,128)}, f32[1,1024]{1,0:T(1,128)S(1)}, u32[]{:S(2)}) copy-start(f32[1,1024]{1,0:T(1,128)S(1)} %get-tuple-element.990) | copy-start | bytes 12292
  19.4 51.9 %copy-start.56 = (f32[1,1024]{1,0:T(1,128)}, f32[1,1024]{1,0:T(1,128)S(1)}, u32[]{:S(2)}) copy-start(f32[1,1024]{1,0:T(1,128)S(1)} %get-tuple-element.992) | copy-start | bytes 12292
  19.4 51.9 %copy-start.59 = (f32[1,1024]{1,0:T(1,128)}, f32[1,1024]{1,0:T(1,128)S(1)}, u32[]{:S(2)}) copy-start(f32[1,1024]{1,0:T(1,128)S(1)} %get-tuple-element.994) | copy-start | bytes 12292
  19.4 51.9 %copy-start.62 = (f32[1,1024]{1,0:T(1,128)}, f32[1,1024]{1,0:T(1,128)S(1)}, u32[]{:S(2)}) copy-start(f32[1,1024]{1,0:T(1,128)S(1)} %get-tuple-element.996) | copy-start | bytes 12292
  19.4 51.9 %copy-start.65 = (f32[1,1024]{1,0:T(1,128)}, f32[1,1024]{1,0:T(1,128)S(1)}, u32[]{:S(2)}) copy-start(f32[1,1024]{1,0:T(1,128)S(1)} %get-tuple-element.998) | copy-start | bytes 12292
  19.4 51.9 %copy-start.123 = (f32[1,1024]{1,0:T(1,128)}, f32[1,1024]{1,0:T(1,128)S(1)}, u32[]{:S(2)}) copy-start(f32[1,1024]{1,0:T(1,128)S(1)} %get-tuple-element.982) | copy-start | bytes 12292
  19.4 51.9 %copy-start.188 = (f32[1,1024]{1,0:T(1,128)}, f32[1,1024]{1,0:T(1,128)S(1)}, u32[]{:S(2)}) copy-start(f32[1,1024]{1,0:T(1,128)S(1)} %get-tuple-element.989) | copy-start | bytes 12292
  19.5 51.9 %copy-start.190 = (f32[1,1024]{1,0:T(1,128)}, f32[1,1024]{1,0:T(1,128)S(1)}, u32[]{:S(2)}) copy-start(f32[1,1024]{1,0:T(1,128)S(1)} %get-tuple-element.993) | copy-start | bytes 12292
  19.5 51.9 %copy-start.192 = (f32[1,1024]{1,0:T(1,128)}, f32[1,1024]{1,0:T(1,128)S(1)}, u32[]{:S(2)}) copy-start(f32[1,1024]{1,0:T(1,128)S(1)} %get-tuple-element.997) | copy-start | bytes 12292
  19.5 51.6 %copy-start = (f32[2,80,512]{2,1,0:T(8,128)S(1)}, f32[2,80,512]{2,1,0:T(8,128)}, u32[]{:S(2)}) copy-start(f32[2,80,512]{2,1,0:T(8,128)} %param.26) | copy-start | bytes 983044
  21.4 50.0 %copy-start.68 = (f32[1,1024]{1,0:T(1,128)}, f32[1,1024]{1,0:T(1,128)S(1)}, u32[]{:S(2)}) copy-start(f32[1,1024]{1,0:T(1,128)S(1)} %get-tuple-element.1001) | copy-start | bytes 12292
  21.4 50.0 %copy-start.71 = (f32[1,1024]{1,0:T(1,128)}, f32[1,1024]{1,0:T(1,128)S(1)}, u32[]{:S(2)}) copy-start(f32[1,1024]{1,0:T(1,128)S(1)} %get-tuple-element.1003) | copy-start | bytes 12292
  21.5 50.0 %copy-start.74 = (f32[1,1024]{1,0:T(1,128)}, f32[1,1024]{1,0:T(1,128)S(1)}, u32[]{:S(2)}) copy-start(f32[1,1024]{1,0:T(1,128)S(1)} %get-tuple-element.1005) | copy-start | bytes 12292
  21.5 50.0 %copy-start.77 = (f32[1,1024]{1,0:T(1,128)}, f32[1,1024]{1,0:T(1,128)S(1)}, u32[]{:S(2)}) copy-start(f32[1,1024]{1,0:T(1,128)S(1)} %get-tuple-element.1007) | copy-start | bytes 12292
  21.5 50.0 %copy-start.80 = (f32[1,1024]{1,0:T(1,128)}, f32[1,1024]{1,0:T(1,128)S(1)}, u32[]{:S(2)}) copy-start(f32[1,1024]{1,0:T(1,128)S(1)} %get-tuple-element.1009) | copy-start | bytes 12292
  21.5 50.0 %copy-start.83 = (f32[1,1024]{1,0:T(1,128)}, f32[1,1024]{1,0:T(1,128)S(1)}, u32[]{:S(2)}) copy-start(f32[1,1024]{1,0:T(1,128)S(1)} %get-tuple-element.1011) | copy-start | bytes 12292
  21.5 50.0 %copy-start.86 = (f32[1,1024]{1,0:T(1,128)}, f32[1,1024]{1,0:T(1,128)S(1)}, u32[]{:S(2)}) copy-start(f32[1,1024]{1,0:T(1,128)S(1)} %get-tuple-element.1013) | copy-start | bytes 12292
  21.5 50.0 %copy-start.89 = (f32[1,1024]{1,0:T(1,128)}, f32[1,1024]{1,0:T(1,128)S(1)}, u32[]{:S(2)}) copy-start(f32[1,1024]{1,0:T(1,128)S(1)} %get-tuple-element.1015) | copy-start | bytes 12292
  21.5 50.0 %copy-start.92 = (f32[1,1024]{1,0:T(1,128)}, f32[1,1024]{1,0:T(1,128)S(1)}, u32[]{:S(2)}) copy-start(f32[1,1024]{1,0:T(1,128)S(1)} %get-tuple-element.1017) | copy-start | bytes 12292
  23.3 48.2 %copy-start.95 = (f32[1,1024]{1,0:T(1,128)}, f32[1,1024]{1,0:T(1,128)S(1)}, u32[]{:S(2)}) copy-start(f32[1,1024]{1,0:T(1,128)S(1)} %get-tuple-element.1020) | copy-start | bytes 12292
  23.3 48.2 %copy-start.98 = (f32[1,1024]{1,0:T(1,128)}, f32[1,1024]{1,0:T(1,128)S(1)}, u32[]{:S(2)}) copy-start(f32[1,1024]{1,0:T(1,128)S(1)} %get-tuple-element.1022) | copy-start | bytes 12292
  23.3 48.2 %copy-start.101 = (f32[1,1024]{1,0:T(1,128)}, f32[1,1024]{1,0:T(1,128)S(1)}, u32[]{:S(2)}) copy-start(f32[1,1024]{1,0:T(1,128)S(1)} %get-tuple-element.1024) | copy-start | bytes 12292
  23.3 48.2 %copy-start.104 = (f32[1,1024]{1,0:T(1,128)}, f32[1,1024]{1,0:T(1,128)S(1)}, u32[]{:S(2)}) copy-start(f32[1,1024]{1,0:T(1,128)S(1)} %get-tuple-element.1026) | copy-start | bytes 12292
  108.2 9.5 %collective-permute-start.3 = (f32[8,4096]{1,0:T(8,128)S(1)}, f32[8,4096]{1,0:T(8,128)S(1)}, u32[]{:S(2)}, u32[]{:S(2)}) collective-permute-start(f32[8,4096]{1,0:T(8,128)S(1)} %all_gather.13), channel_id=1, source_target_pairs={{4,0},{8,4},{12,8},{16,12},{20,16},{24,20},{28,24},{0,28},{5,1},{9... | collective-permute-start | bytes 393224 | tf_op jit(solution)/shard_map/ppermute | solution.py:17
  108.2 9.5 %collective-permute-start.2 = (f32[8,4096]{1,0:T(8,128)S(1)}, f32[8,4096]{1,0:T(8,128)S(1)}, u32[]{:S(2)}, u32[]{:S(2)}) collective-permute-start(f32[8,4096]{1,0:T(8,128)S(1)} %all_gather.13), channel_id=1, source_target_pairs={{0,4},{4,8},{8,12},{12,16},{16,20},{20,24},{24,28},{28,0},{1,5},{5... | collective-permute-start | bytes 393224 | tf_op jit(solution)/shard_map/ppermute | solution.py:16
  149.0 1.4 collective-permute-start.5
  149.0 4.2 %collective-permute-start.4 = (f32[2,2048]{1,0:T(2,128)S(1)}, f32[2,2048]{1,0:T(2,128)S(1)}, u32[]{:S(2)}, u32[]{:S(2)}) collective-permute-start(f32[2,2048]{1,0:T(2,128)S(1)} %all_gather.14), channel_id=1, source_target_pairs={{0,4},{4,8},{8,12},{12,16},{16,20},{20,24},{24,28},{28,0},{1,5},{5... | collective-permute-start | bytes 49160 | tf_op jit(solution)/shard_map/ppermute | solution.py:16
  189.6 34.3 %collective-permute-start.7 = (f32[8,4096]{1,0:T(8,128)S(1)}, f32[8,4096]{1,0:T(8,128)S(1)}, u32[]{:S(2)}, u32[]{:S(2)}) collective-permute-start(f32[8,4096]{1,0:T(8,128)S(1)} %all_gather.15), channel_id=1, source_target_pairs={{4,0},{8,4},{12,8},{16,12},{20,16},{24,20},{28,24},{0,28},{5,1},{9... | collective-permute-start | bytes 393224 | tf_op jit(solution)/shard_map/ppermute | solution.py:17
  189.6 34.3 %collective-permute-start.6 = (f32[8,4096]{1,0:T(8,128)S(1)}, f32[8,4096]{1,0:T(8,128)S(1)}, u32[]{:S(2)}, u32[]{:S(2)}) collective-permute-start(f32[8,4096]{1,0:T(8,128)S(1)} %all_gather.15), channel_id=1, source_target_pairs={{0,4},{4,8},{8,12},{12,16},{16,20},{20,24},{24,28},{28,0},{1,5},{5... | collective-permute-start | bytes 393224 | tf_op jit(solution)/shard_map/ppermute | solution.py:16
  (197 other events, 2799.1 us)
where the time goes:
time: 247 us; the launch traced here: 243 us
  other arithmetic  91.4 us (37%)
  local copies, waits for them, and re-layouts  86.3 us (35%)
  blocking collectives  55.1 us (22%)
  between operations  5.39 us (2%)
  waiting for transfers between devices  3.08 us (1%)
    gather x4, local copies, waits for them, and re-layouts, remap(): return jnp.sum(weights[None] * values[:, places], axis=1)  47.4 us
    unnamed x114, other arithmetic  28.9 us
    all_gather x2, blocking collectives, per_device(): sea_block = lax.all_gather(sea_top, 'col', axis=1, tiled=True)  28.1 us
    all_gather x2, blocking collectives, per_device(): flux_block = lax.all_gather(fluxes, 'col', axis=1, tiled=True)  27 us
    add x22, other arithmetic, solve_columns(): pivot_value = 1.0 + lower_k + upper_k + lower_k * carry_c  26.1 us
    slice x4, local copies, waits for them, and re-layouts, solve_columns(): carry_d = (right_side[:, depth_index] + lower_k * carry_d) / pivot_value  12.2 us
    concatenate x4, local copies, waits for them, and re-layouts, extended(): value = jnp.concatenate([before, value, after], axis=dim)  11.7 us
    div x8, other arithmetic, solve_columns(): carry_d = (right_side[:, depth_index] + lower_k * carry_d) / pivot_value  10.5 us
  transfers between devices with their start and end apart: 8, of which 2 were waited for; matrix products, arithmetic and copies ran while one was open for 39% of the time, Pallas kernels for 0%

commit v1 on v0

--- a/solution.py
+++ b/solution.py
@@ -109,7 +109,14 @@
     air_span = air_cols * group_count
     for step_index in range(STEPS):
         sea_top = jnp.stack([sea_state[0, 0], ice_cover])
-        sea_block = lax.all_gather(sea_top, "col", axis=1, tiled=True)
+        ring = [sea_top]
+        for hop in range(3):
+            ring.append(lax.ppermute(ring[-1], "col", [(dev, (dev + 1) % 4) for dev in range(4)]))
+        sea_block = jnp.roll(
+            jnp.concatenate(ring[::-1], axis=1),
+            (lax.axis_index("col") + 1) * ring[0].shape[1],
+            axis=1,
+        )
         sea_nearby = extended(sea_block, (("sec", 1),), sea_cols * group_count)
         air_sea = remap(sea_nearby, ocean_sources, ocean_weights)
         fluxes = surface_fluxes(air_state, air_sea, surface_forcing, air_mask)

time: 247 us -> 241 us (0.976)
  blocking collectives: 55.1 us -> 26.8 us
  waiting for transfers between devices: 3.08 us -> 26.1 us
  other arithmetic: 91.4 us -> 84.6 us
  starting transfers between devices: 2.04 us -> 7.06 us
    all_gather x2 -> x0, blocking collectives: 28.1 us -> none  [per_device(): sea_block = lax.all_gather(sea_top, 'col', axis=1, tiled=True)]
    ppermute x0 -> x6, waiting for transfers between devices: none -> 15.1 us  [per_device(): lax.ppermute(ring[-1], 'col', [(dev, (dev + 1) % 4) for dev in range(4)])]
    ppermute x0 -> x6, starting transfers between devices: none -> 4.93 us  [per_device(): lax.ppermute(ring[-1], 'col', [(dev, (dev + 1) % 4) for dev in range(4)])]
    ppermute x4, waiting for transfers between devices: 2.75 us -> 7.42 us  [extended(): before = lax.ppermute(last, axis, up)]
    unnamed x114, other arithmetic: 28.9 us -> 24.8 us
    ppermute x4, waiting for transfers between devices: 0.33 us -> 3.66 us  [extended(): after = lax.ppermute(leading, axis, down)]
    unnamed x555 -> x563, local copies, waits for them, and re-layouts: 4.5 us -> 5.12 us
  transfers between devices with their start and end apart: 8 -> 14, of which waited for: 2 -> 11; matrix products, arithmetic and copies ran while one was open for 39% -> 38% of each run, Pallas kernels for 0% -> 0%
where the time goes in v1:
time: 241 us; the launch traced here: 237 us
  local copies, waits for them, and re-layouts  86.7 us (36%)
  other arithmetic  84.6 us (35%)
  blocking collectives  26.8 us (11%)
  waiting for transfers between devices  26.1 us (11%)
  starting transfers between devices  7.06 us (3%)
  between operations  5.44 us (2%)
    gather x4, local copies, waits for them, and re-layouts, remap(): return jnp.sum(weights[None] * values[:, places], axis=1)  47.3 us
    all_gather x2, blocking collectives, per_device(): flux_block = lax.all_gather(fluxes, 'col', axis=1, tiled=True)  26.8 us
    add x22, other arithmetic, solve_columns(): pivot_value = 1.0 + lower_k + upper_k + lower_k * carry_c  26.5 us
    unnamed x114, other arithmetic  24.8 us
    ppermute x6, waiting for transfers between devices, per_device(): lax.ppermute(ring[-1], 'col', [(dev, (dev + 1) % 4) for dev in range(4)])  15.1 us
    slice x4, local copies, waits for them, and re-layouts, solve_columns(): carry_d = (right_side[:, depth_index] + lower_k * carry_d) / pivot_value  12.2 us
    concatenate x4, local copies, waits for them, and re-layouts, extended(): value = jnp.concatenate([before, value, after], axis=dim)  11.6 us
    div x8, other arithmetic, solve_columns(): carry_d = (right_side[:, depth_index] + lower_k * carry_d) / pivot_value  10.2 us
  transfers between devices with their start and end apart: 14, of which 11 were waited for; matrix products, arithmetic and copies ran while one was open for 38% of the time, Pallas kernels for 0%

profile of v1, /device:TPU:0, one launch (start us, length us, event | category | flops | bytes accessed | tf_op | source)
XLA Modules:
  0.0 236.7 jit_solution(12256113815769741698)
XLA Ops:
  2.1 3.1 %collective-permute-start = (f32[2,512]{1,0:T(2,128)S(1)}, f32[2,512]{1,0:T(2,128)S(1)}, u32[]{:S(2)}, u32[]{:S(2)}) collective-permute-start(f32[2,512]{1,0:T(2,128)S(1)} %pad_maximum_fusion.4), channel_id=1, source_target_pairs={{0,1},{1,2},{2,3},{3,0},{4,5},{5,6},{6,7},{7,4},{8,9},{9,10},{10,1... | collective-permute-start | bytes 12296 | tf_op jit(solution)/shard_map/ppermute | solution.py:114
  7.1 1.9 fusion.476
  10.9 2.9 %negate_divide_fusion.20 = (f32[1,1024]{1,0:T(1,128)}, f32[1,1024]{1,0:T(1,128)}, f32[1,1024]{1,0:T(1,128)}, f32[1,1024]{1,0:T(1,128)}, f32[1,1024]{1,0:T(1,128)...) fusion(f32[64,1024]{1,0:T(8,128)} %param.23), kind=kLoop, calls=%fused_computation.1354 | loop fusion | flops 260096 | bytes 524288 | tf_op jit(solution)/shard_map/div | solution.py:33
  13.8 3.2 %fusion.470 = (f32[4,1,1024]{2,1,0:T(1,128)S(1)}, f32[4,1,1024]{2,1,0:T(1,128)}, f32[4,1,1024]{2,1,0:T(1,128)}, f32[4,1,1024]{2,1,0:T(1,128)}, f32[4,1,1024]{2,1...) fusion(f32[4,64,1024]{2,1,0:T(8,128)} %param.22), kind=kLoop, calls=%fused_computation.1800 | loop fusion | bytes 622592 | tf_op jit(solution)/shard_map/slice | solution.py:34
  17.1 3.4 %fusion.471 = (f32[4,1,1024]{2,1,0:T(1,128)}, f32[4,1,1024]{2,1,0:T(1,128)}, f32[4,1,1024]{2,1,0:T(1,128)S(1)}, f32[4,1,1024]{2,1,0:T(1,128)}, f32[4,1,1024]{2,1...) fusion(f32[4,64,1024]{2,1,0:T(8,128)} %param.22), kind=kLoop, calls=%fused_computation.1801 | loop fusion | bytes 622592 | tf_op jit(solution)/shard_map/slice | solution.py:34
  20.6 2.0 fusion.474
  24.0 2.3 fusion.472
  26.3 3.3 %fusion.469 = (f32[4,1,1024]{2,1,0:T(1,128)}, f32[4,1,1024]{2,1,0:T(1,128)S(1)}, f32[4,1,1024]{2,1,0:T(1,128)}, f32[4,1,1024]{2,1,0:T(1,128)}, f32[4,1,1024]{2,1...) fusion(f32[4,64,1024]{2,1,0:T(8,128)} %param.22), kind=kLoop, calls=%fused_computation.1799 | loop fusion | bytes 622592 | tf_op jit(solution)/shard_map/slice | solution.py:34
  58.9 2.5 %collective-permute-done.1 = f32[2,512]{1,0:T(2,128)S(1)} collective-permute-done((f32[2,512]{1,0:T(2,128)S(1)}, f32[2,512]{1,0:T(2,128)S(1)}, u32[]{:S(2)}, u32[]{:S(2)}) %collective-permute-start.1) | collective-permute-done | bytes 4128 | tf_op jit(solution)/shard_map/ppermute | solution.py:114
  62.1 4.7 %collective-permute-done.2 = f32[2,512]{1,0:T(2,128)S(1)} collective-permute-done((f32[2,512]{1,0:T(2,128)S(1)}, f32[2,512]{1,0:T(2,128)S(1)}, u32[]{:S(2)}, u32[]{:S(2)}) %collective-permute-start.2) | collective-permute-done | bytes 4128 | tf_op jit(solution)/shard_map/ppermute | solution.py:114
  68.6 2.8 %collective-permute-done.3 = f32[2,2048]{1,0:T(2,128)S(1)} collective-permute-done((f32[2,2048]{1,0:T(2,128)S(1)}, f32[2,2048]{1,0:T(2,128)S(1)}, u32[]{:S(2)}, u32[]{:S(2)}) %collective-permute-start.3) | collective-permute-done | bytes 16416 | tf_op jit(solution)/shard_map/ppermute | solution.py:16
  73.8 15.4 %gather_fusion = f32[4096,2]{1,0:T(8,128)} fusion(f32[2,6144]{0,1:T(8,128)S(1)} %copy.754, s32[4096]{0:T(1024)} %bitcast_clamp_fusion), kind=kCustom, calls=%fused_computation | custom fusion | bytes 81920 | tf_op jit(solution)/shard_map/gather | solution.py:46
  89.3 2.0 multiply_reduce_fusion.1
  92.0 13.4 %all_gather.6 = f32[8,4096]{1,0:T(8,128)S(1)} all-gather(f32[8,1024]{1,0:T(8,128)S(1)} %stack.715), channel_id=1, replica_groups=mesh['sec'=8,'col'=4] {'col'}, dimensions={1}, use_global_device_ids=true | all-gather | bytes 163840 | tf_op jit(solution)/shard_map/all_gather | solution.py:123
  106.3 3.0 %collective-permute-done.6 = f32[8,4096]{1,0:T(8,128)S(1)} collective-permute-done((f32[8,4096]{1,0:T(8,128)S(1)}, f32[8,4096]{1,0:T(8,128)S(1)}, u32[]{:S(2)}, u32[]{:S(2)}) %collective-permute-start.6) | collective-permute-done | bytes 131104 | tf_op jit(solution)/shard_map/ppermute | solution.py:17
  109.3 1.9 collective-permute-done.5
  111.2 3.9 %copy.819 = f32[8,12288]{0,1:T(8,128)} copy(f32[8,12288]{1,0:T(8,128)S(1)} %pad_maximum_fusion) | data formatting | bytes 786432 | tf_op jit(solution)/shard_map/concatenate | solution.py:18
  115.2 8.3 %gather_fusion.1 = f32[2048,8]{1,0:T(8,128)S(1)} fusion(f32[8,12288]{0,1:T(8,128)} %copy.819, s32[2048]{0:T(1024)S(1)} %broadcast_clamp_fusion), kind=kCustom, calls=%fused_computation.1 | custom fusion | bytes 139264 | tf_op jit(solution)/shard_map/gather | solution.py:46
  132.0 3.3 %collective-permute-done.7 = f32[2,512]{1,0:T(2,128)S(1)} collective-permute-done((f32[2,512]{1,0:T(2,128)S(1)}, f32[2,512]{1,0:T(2,128)S(1)}, u32[]{:S(2)}, u32[]{:S(2)}) %collective-permute-start.7) | collective-permute-done | bytes 4128 | tf_op jit(solution)/shard_map/ppermute | solution.py:114
  135.7 3.6 %multiply_subtract_fusion.103 = (f32[4,1024]{1,0:T(4,128)S(1)}, f32[4,1024]{1,0:T(4,128)}, f32[4,1024]{1,0:T(4,128)}, f32[4,1024]{1,0:T(4,128)}, f32[4,1024]{1,0...) fusion(f32[4,1024]{1,0:T(4,128)S(1)} %get-tuple-element.743, ...), kind=kLoop, calls=%fused_computation.750 | loop fusion | flops 1200128 | bytes 2097152 | tf_op jit(solution)/shard_map/sub | solution.py:40
  141.6 2.0 add_divide_fusion.63
  143.6 2.8 %collective-permute-done.9 = f32[2,512]{1,0:T(2,128)S(1)} collective-permute-done((f32[2,512]{1,0:T(2,128)S(1)}, f32[2,512]{1,0:T(2,128)S(1)}, u32[]{:S(2)}, u32[]{:S(2)}) %collective-permute-start.9) | collective-permute-done | bytes 4128 | tf_op jit(solution)/shard_map/ppermute | solution.py:114
  148.1 2.7 %collective-permute-done.10 = f32[2,2048]{1,0:T(2,128)S(1)} collective-permute-done((f32[2,2048]{1,0:T(2,128)S(1)}, f32[2,2048]{1,0:T(2,128)S(1)}, u32[]{:S(2)}, u32[]{:S(2)}) %collective-permute-start.10) | collective-permute-done | bytes 16416 | tf_op jit(solution)/shard_map/ppermute | solution.py:16
  153.2 15.4 %gather_fusion.2 = f32[4096,2]{1,0:T(8,128)} fusion(f32[2,6144]{0,1:T(8,128)S(1)} %copy.901, s32[4096]{0:T(1024)} %bitcast_clamp_fusion), kind=kCustom, calls=%fused_computation.2 | custom fusion | bytes 81920 | tf_op jit(solution)/shard_map/gather | solution.py:46
  169.0 2.0 multiply_reduce_fusion
  173.8 13.4 %all_gather.7 = f32[8,4096]{1,0:T(8,128)S(1)} all-gather(f32[8,1024]{1,0:T(8,128)S(1)} %stack.831), channel_id=1, replica_groups=mesh['sec'=8,'col'=4] {'col'}, dimensions={1}, use_global_device_ids=true | all-gather | bytes 163840 | tf_op jit(solution)/shard_map/all_gather | solution.py:123
  188.0 3.1 %add_divide_fusion.38 = (f32[4,1,1024]{2,0,1:T(4,128)S(1)}, f32[4,1,1024]{2,0,1:T(4,128)S(1)}, f32[4,1,1024]{2,0,1:T(4,128)S(1)}, f32[4,1,1024]{2,0,1:T(4,128)S(...) fusion(f32[1024]{0:T(1024)} %bitcast.3426, ...), kind=kLoop, calls=%fused_computation.624 | loop fusion | flops 1093632 | bytes 2232320 | tf_op jit(solution)/shard_map/div | solution.py:34
  191.5 2.0 add_divide_fusion.60
  193.5 2.6 %constant_dynamic-update-slice_fusion.143 = (f32[4,64,1024]{2,0,1:T(4,128)S(1)}, f32[4,1024]{1,0:T(4,128)S(1)}, f32[4,1024]{1,0:T(4,128)S(1)}, f32[4,1024]{1,0:T...) fusion(f32[4,1024]{1,0:T(4,128)S(1)} %get-tuple-element.438, ...), kind=kLoop, calls=%fused_computation.155 | loop fusion | flops 1392639 | bytes 2138112
  196.5 3.4 %constant_dynamic-update-slice_fusion.142 = (f32[4,64,1024]{2,0,1:T(4,128)S(1)}, f32[4,1,1024]{2,0,1:T(4,128)S(1)}, f32[4,1,1024]{2,0,1:T(4,128)S(1)}, f32[4,1,1...) fusion(f32[4,64,1024]{2,0,1:T(4,128)S(1)} %get-tuple-element.40, ...), kind=kLoop, calls=%fused_computation.154 | loop fusion | flops 1454080 | bytes 2519040
  217.4 4.1 %copy.902 = f32[8,12288]{0,1:T(8,128)} copy(f32[8,12288]{1,0:T(8,128)S(1)} %pad_maximum_fusion.1) | data formatting | bytes 786432 | tf_op jit(solution)/shard_map/concatenate | solution.py:18
  221.6 8.3 %gather_fusion.3 = f32[2048,8]{1,0:T(8,128)S(1)} fusion(f32[8,12288]{0,1:T(8,128)} %copy.902, s32[2048]{0:T(1024)S(1)} %copy-done.200), kind=kCustom, calls=%fused_computation.3 | custom fusion | bytes 139264 | tf_op jit(solution)/shard_map/gather | solution.py:46
  (850 shorter events, 82.6 us)
Async XLA Ops:
  2.1 54.0 %collective-permute-start = (f32[2,512]{1,0:T(2,128)S(1)}, f32[2,512]{1,0:T(2,128)S(1)}, u32[]{:S(2)}, u32[]{:S(2)}) collective-permute-start(f32[2,512]{1,0:T(2,128)S(1)} %pad_maximum_fusion.4), channel_id=1, source_target_pairs={{0,1},{1,2},{2,3},{3,0},{4,5},{5,6},{6,7},{7,4},{8,9},{9,10},{10,1... | collective-permute-start | bytes 12296 | tf_op jit(solution)/shard_map/ppermute | solution.py:114
  7.0 134.0 %copy-start.49 = (f32[1,1024]{1,0:T(1,128)}, f32[1,1024]{1,0:T(1,128)S(1)}, u32[]{:S(2)}) copy-start(f32[1,1024]{1,0:T(1,128)S(1)} %get-tuple-element.989) | copy-start | bytes 12292
  7.0 134.0 %copy-start.51 = (f32[1,1024]{1,0:T(1,128)}, f32[1,1024]{1,0:T(1,128)S(1)}, u32[]{:S(2)}) copy-start(f32[1,1024]{1,0:T(1,128)S(1)} %get-tuple-element.991) | copy-start | bytes 12292
  7.0 134.0 %copy-start.53 = (f32[1,1024]{1,0:T(1,128)}, f32[1,1024]{1,0:T(1,128)S(1)}, u32[]{:S(2)}) copy-start(f32[1,1024]{1,0:T(1,128)S(1)} %get-tuple-element.993) | copy-start | bytes 12292
  7.0 134.0 %copy-start.55 = (f32[1,1024]{1,0:T(1,128)}, f32[1,1024]{1,0:T(1,128)S(1)}, u32[]{:S(2)}) copy-start(f32[1,1024]{1,0:T(1,128)S(1)} %get-tuple-element.995) | copy-start | bytes 12292
  7.0 134.0 %copy-start.57 = (f32[1,1024]{1,0:T(1,128)}, f32[1,1024]{1,0:T(1,128)S(1)}, u32[]{:S(2)}) copy-start(f32[1,1024]{1,0:T(1,128)S(1)} %get-tuple-element.997) | copy-start | bytes 12292
  7.0 134.0 %copy-start.59 = (f32[1,1024]{1,0:T(1,128)}, f32[1,1024]{1,0:T(1,128)S(1)}, u32[]{:S(2)}) copy-start(f32[1,1024]{1,0:T(1,128)S(1)} %get-tuple-element.999) | copy-start | bytes 12292
  9.0 120.8 %copy-start.65 = (f32[1,1024]{1,0:T(1,128)}, f32[1,1024]{1,0:T(1,128)S(1)}, u32[]{:S(2)}) copy-start(f32[1,1024]{1,0:T(1,128)S(1)} %get-tuple-element.1006) | copy-start | bytes 12292
  9.1 120.8 %copy-start.68 = (f32[1,1024]{1,0:T(1,128)}, f32[1,1024]{1,0:T(1,128)S(1)}, u32[]{:S(2)}) copy-start(f32[1,1024]{1,0:T(1,128)S(1)} %get-tuple-element.1008) | copy-start | bytes 12292
  9.1 120.8 %copy-start.71 = (f32[1,1024]{1,0:T(1,128)}, f32[1,1024]{1,0:T(1,128)S(1)}, u32[]{:S(2)}) copy-start(f32[1,1024]{1,0:T(1,128)S(1)} %get-tuple-element.1010) | copy-start | bytes 12292
  9.1 132.0 %copy-start.61 = (f32[1,1024]{1,0:T(1,128)}, f32[1,1024]{1,0:T(1,128)S(1)}, u32[]{:S(2)}) copy-start(f32[1,1024]{1,0:T(1,128)S(1)} %get-tuple-element.1002) | copy-start | bytes 12292
  9.1 132.0 %copy-start.63 = (f32[1,1024]{1,0:T(1,128)}, f32[1,1024]{1,0:T(1,128)S(1)}, u32[]{:S(2)}) copy-start(f32[1,1024]{1,0:T(1,128)S(1)} %get-tuple-element.1004) | copy-start | bytes 12292
  17.0 124.1 %copy-start.5 = (f32[4,1,1024]{2,1,0:T(1,128)}, f32[4,1,1024]{2,1,0:T(1,128)S(1)}, u32[]{:S(2)}) copy-start(f32[4,1,1024]{2,1,0:T(1,128)S(1)} %get-tuple-element.920) | copy-start | bytes 49156
  17.0 124.1 %copy-start.7 = (f32[4,1,1024]{2,1,0:T(1,128)}, f32[4,1,1024]{2,1,0:T(1,128)S(1)}, u32[]{:S(2)}) copy-start(f32[4,1,1024]{2,1,0:T(1,128)S(1)} %get-tuple-element.922) | copy-start | bytes 49156
  17.0 124.1 %copy-start.9 = (f32[4,1,1024]{2,1,0:T(1,128)}, f32[4,1,1024]{2,1,0:T(1,128)S(1)}, u32[]{:S(2)}) copy-start(f32[4,1,1024]{2,1,0:T(1,128)S(1)} %get-tuple-element.924) | copy-start | bytes 49156
  17.0 124.1 %copy-start.11 = (f32[4,1,1024]{2,1,0:T(1,128)}, f32[4,1,1024]{2,1,0:T(1,128)S(1)}, u32[]{:S(2)}) copy-start(f32[4,1,1024]{2,1,0:T(1,128)S(1)} %get-tuple-element.926) | copy-start | bytes 49156
  17.0 124.1 %copy-start.13 = (f32[4,1,1024]{2,1,0:T(1,128)}, f32[4,1,1024]{2,1,0:T(1,128)S(1)}, u32[]{:S(2)}) copy-start(f32[4,1,1024]{2,1,0:T(1,128)S(1)} %get-tuple-element.928) | copy-start | bytes 49156
  17.1 124.1 %copy-start.15 = (f32[4,1,1024]{2,1,0:T(1,128)}, f32[4,1,1024]{2,1,0:T(1,128)S(1)}, u32[]{:S(2)}) copy-start(f32[4,1,1024]{2,1,0:T(1,128)S(1)} %get-tuple-element.930) | copy-start | bytes 49156
  17.1 124.1 %copy-start.17 = (f32[4,1,1024]{2,1,0:T(1,128)}, f32[4,1,1024]{2,1,0:T(1,128)S(1)}, u32[]{:S(2)}) copy-start(f32[4,1,1024]{2,1,0:T(1,128)S(1)} %get-tuple-element.932) | copy-start | bytes 49156
  56.0 5.4 %collective-permute-start.1 = (f32[2,512]{1,0:T(2,128)S(1)}, f32[2,512]{1,0:T(2,128)S(1)}, u32[]{:S(2)}, u32[]{:S(2)}) collective-permute-start(f32[2,512]{1,0:T(2,128)S(1)} %collective-permute-done), channel_id=1, source_target_pairs={{0,1},{1,2},{2,3},{3,0},{4,5},{5,6},{6,7},{7,4},{8,9},{9,10},{10,1... | collective-permute-start | bytes 12296 | tf_op jit(solution)/shard_map/ppermute | solution.py:114
  61.4 5.4 %collective-permute-start.2 = (f32[2,512]{1,0:T(2,128)S(1)}, f32[2,512]{1,0:T(2,128)S(1)}, u32[]{:S(2)}, u32[]{:S(2)}) collective-permute-start(f32[2,512]{1,0:T(2,128)S(1)} %collective-permute-done.1), channel_id=1, source_target_pairs={{0,1},{1,2},{2,3},{3,0},{4,5},{5,6},{6,7},{7,4},{8,9},{9,10},{10,1... | collective-permute-start | bytes 12296 | tf_op jit(solution)/shard_map/ppermute | solution.py:114
  67.1 1.5 collective-permute-start.4
  67.1 4.3 %collective-permute-start.3 = (f32[2,2048]{1,0:T(2,128)S(1)}, f32[2,2048]{1,0:T(2,128)S(1)}, u32[]{:S(2)}, u32[]{:S(2)}) collective-permute-start(f32[2,2048]{1,0:T(2,128)S(1)} %fusion.12), channel_id=1, source_target_pairs={{0,4},{4,8},{8,12},{12,16},{16,20},{20,24},{24,28},{28,0},{1,5},{5... | collective-permute-start | bytes 49160 | tf_op jit(solution)/shard_map/ppermute | solution.py:16
  105.4 3.8 %collective-permute-start.6 = (f32[8,4096]{1,0:T(8,128)S(1)}, f32[8,4096]{1,0:T(8,128)S(1)}, u32[]{:S(2)}, u32[]{:S(2)}) collective-permute-start(f32[8,4096]{1,0:T(8,128)S(1)} %all_gather.6), channel_id=1, source_target_pairs={{4,0},{8,4},{12,8},{16,12},{20,16},{24,20},{28,24},{0,28},{5,1},{9... | collective-permute-start | bytes 393224 | tf_op jit(solution)/shard_map/ppermute | solution.py:17
  105.4 5.8 %collective-permute-start.5 = (f32[8,4096]{1,0:T(8,128)S(1)}, f32[8,4096]{1,0:T(8,128)S(1)}, u32[]{:S(2)}, u32[]{:S(2)}) collective-permute-start(f32[8,4096]{1,0:T(8,128)S(1)} %all_gather.6), channel_id=1, source_target_pairs={{0,4},{4,8},{8,12},{12,16},{16,20},{20,24},{24,28},{28,0},{1,5},{5... | collective-permute-start | bytes 393224 | tf_op jit(solution)/shard_map/ppermute | solution.py:16
  129.6 5.6 %collective-permute-start.7 = (f32[2,512]{1,0:T(2,128)S(1)}, f32[2,512]{1,0:T(2,128)S(1)}, u32[]{:S(2)}, u32[]{:S(2)}) collective-permute-start(f32[2,512]{1,0:T(2,128)S(1)} %pad_maximum_fusion.5), channel_id=1, source_target_pairs={{0,1},{1,2},{2,3},{3,0},{4,5},{5,6},{6,7},{7,4},{8,9},{9,10},{10,1... | collective-permute-start | bytes 12296 | tf_op jit(solution)/shard_map/ppermute | solution.py:114
  135.5 5.5 %collective-permute-start.8 = (f32[2,512]{1,0:T(2,128)S(1)}, f32[2,512]{1,0:T(2,128)S(1)}, u32[]{:S(2)}, u32[]{:S(2)}) collective-permute-start(f32[2,512]{1,0:T(2,128)S(1)} %collective-permute-done.7), channel_id=1, source_target_pairs={{0,1},{1,2},{2,3},{3,0},{4,5},{5,6},{6,7},{7,4},{8,9},{9,10},{10,1... | collective-permute-start | bytes 12296 | tf_op jit(solution)/shard_map/ppermute | solution.py:114
  141.0 5.4 %collective-permute-start.9 = (f32[2,512]{1,0:T(2,128)S(1)}, f32[2,512]{1,0:T(2,128)S(1)}, u32[]{:S(2)}, u32[]{:S(2)}) collective-permute-start(f32[2,512]{1,0:T(2,128)S(1)} %collective-permute-done.8), channel_id=1, source_target_pairs={{0,1},{1,2},{2,3},{3,0},{4,5},{5,6},{6,7},{7,4},{8,9},{9,10},{10,1... | collective-permute-start | bytes 12296 | tf_op jit(solution)/shard_map/ppermute | solution.py:114
  146.6 1.5 collective-permute-start.11
  146.7 4.1 %collective-permute-start.10 = (f32[2,2048]{1,0:T(2,128)S(1)}, f32[2,2048]{1,0:T(2,128)S(1)}, u32[]{:S(2)}, u32[]{:S(2)}) collective-permute-start(f32[2,2048]{1,0:T(2,128)S(1)} %fusion.3), channel_id=1, source_target_pairs={{0,4},{4,8},{8,12},{12,16},{16,20},{20,24},{24,28},{28,0},{1,5},{5... | collective-permute-start | bytes 49160 | tf_op jit(solution)/shard_map/ppermute | solution.py:16
  187.1 30.2 %collective-permute-start.13 = (f32[8,4096]{1,0:T(8,128)S(1)}, f32[8,4096]{1,0:T(8,128)S(1)}, u32[]{:S(2)}, u32[]{:S(2)}) collective-permute-start(f32[8,4096]{1,0:T(8,128)S(1)} %all_gather.7), channel_id=1, source_target_pairs={{4,0},{8,4},{12,8},{16,12},{20,16},{24,20},{28,24},{0,28},{5,1},{9... | collective-permute-start | bytes 393224 | tf_op jit(solution)/shard_map/ppermute | solution.py:17
  187.1 30.2 %collective-permute-start.12 = (f32[8,4096]{1,0:T(8,128)S(1)}, f32[8,4096]{1,0:T(8,128)S(1)}, u32[]{:S(2)}, u32[]{:S(2)}) collective-permute-start(f32[8,4096]{1,0:T(8,128)S(1)} %all_gather.7), channel_id=1, source_target_pairs={{0,4},{4,8},{8,12},{12,16},{16,20},{20,24},{24,28},{28,0},{1,5},{5... | collective-permute-start | bytes 393224 | tf_op jit(solution)/shard_map/ppermute | solution.py:16
  (207 other events, 3581.0 us)
